TPU v7x, 128 devices: a whole 4x4x4 slice. The times are simulated.
128 devices in a mesh: ctx: 8 (over y, x_hi), head: 16 (over x_lo, z, core).
Axes of the slice: x: 4 (x_hi: 2, x_lo: 2; x = x_hi * 2 + x_lo), y: 4, z: 4, core: 2. Of those that a mesh axis runs over, the one named last changes fastest.
Arguments:
- queries: bfloat16 [2, 4096, 4096], P(None, 'ctx', 'head'), may hold values from -6 to 6
- keys: bfloat16 [2, 4096, 4096], P(None, 'ctx', 'head'), may hold values from -6 to 6
- values: bfloat16 [2, 4096, 4096], P(None, 'ctx', 'head'), may hold values from -6 to 6
- rates: float32 [16, 2, 4096], P('head', None, 'ctx'), may hold values from 0.05 to 1
- w_gate: float32 [16, 256, 512], P('head'), may hold values from -0.375 to 0.375
- w_up: float32 [16, 256, 512], P('head'), may hold values from -0.375 to 0.375
- w_down: float32 [16, 512, 256], P('head'), may hold values from -0.25 to 0.25
- gains: float32 [16, 256], P('head'), may hold values from 0.25 to 0.6
- out_proj: bfloat16 [4096, 4096], P('head'), may hold values from -0.125 to 0.125
Outputs:
- output: bfloat16 [2, 4096, 4096], P(None, 'ctx', 'head')
All inputs are finite; a program needn't handle non-finite values.
Results may differ from a plain program's by a relative error of at most 0.0051.
Values may be sent and summed in bfloat16 or wider, within the bound.
A program may use at most 128 MiB of HBM per device.

v0:
```python
import jax
import jax.numpy as jnp
from jax import lax
from jax.sharding import PartitionSpec as P

WINDOW = 256
NS_ITERS = 5
highest = lax.Precision.HIGHEST
attn_temp = 5.0
step_size = 0.5
quintic_one = 3.4445
quintic_two = -4.775
quintic_three = 2.0315


def passed_along(value, axis, steps):
    count = lax.axis_size(axis)
    pairs = [(source, (source + steps) % count) for source in range(count)]
    return lax.ppermute(value, axis, pairs)


def unit_rows(matrix):
    return matrix / jnp.sqrt(jnp.sum(matrix * matrix, axis=-1, keepdims=True) + 1e-06)


def exact_dot(left, right):
    return jnp.dot(left, right, precision=highest, preferred_element_type=jnp.float32)


def fast_grads(key_unit, value_rows, rate_rows, w_gate, w_up, w_down):
    gate_pre = exact_dot(key_unit, w_gate)
    up_pre = exact_dot(key_unit, w_up)
    sigma = jax.nn.sigmoid(gate_pre)
    gate_act = gate_pre * sigma
    hidden = gate_act * up_pre
    target = rate_rows[:, None] * value_rows
    grad_down = exact_dot(hidden.T, target)
    back_hidden = exact_dot(target, w_down.T)
    slope = sigma * (1.0 + gate_pre * (1.0 - sigma))
    grad_gate = exact_dot(key_unit.T, back_hidden * up_pre * slope)
    grad_up = exact_dot(key_unit.T, back_hidden * gate_act)
    return jnp.stack([grad_gate, grad_up, grad_down.T])


def quintic_step(gram, iterate):
    poly = quintic_two * gram + quintic_three * jnp.einsum(
        "mij,mjk->mik", gram, gram, precision=highest
    )
    return quintic_one * iterate + jnp.einsum("mij,mjk->mik", poly, iterate, precision=highest)


def orthogonal(grads):
    norms = jnp.sqrt(jnp.sum(grads * grads, axis=(1, 2), keepdims=True)) + 1e-06
    iterate = grads / norms
    for sweep_at in range(NS_ITERS):
        gram = jnp.einsum("mik,mjk->mij", iterate, iterate, precision=highest)
        iterate = quintic_step(gram, iterate)
    return iterate


def apply_fast(query_unit, w_gate, w_up, w_down):
    gate_pre = exact_dot(query_unit, w_gate)
    gate_act = gate_pre * jax.nn.sigmoid(gate_pre)
    return exact_dot(gate_act * exact_dot(query_unit, w_up), w_down)


def band_attention(query_half, ext_keys, ext_values, masked_head):
    local_rows = query_half.shape[0]
    block_rows = min(512, local_rows)
    scores = lax.dot_general(
        query_half, ext_keys, (((1,), (1,)), ((), ())), preferred_element_type=jnp.float32
    )
    query_pos = jnp.arange(block_rows, dtype=jnp.int32)[:, None]
    key_pos = jnp.arange(block_rows + WINDOW, dtype=jnp.int32)[None, :]
    distance = query_pos + WINDOW - key_pos
    valid = (distance >= 0) & (distance < WINDOW)
    if masked_head is not None:
        valid = valid & ((key_pos + 0 >= WINDOW) | jnp.logical_not(masked_head))
    weights = jnp.where(valid, jnp.exp(attn_temp * (scores - 1.0)), 0.0)
    probs = (weights / jnp.sum(weights, axis=-1, keepdims=True)).astype(jnp.bfloat16)
    outputs = jnp.dot(probs, ext_values, preferred_element_type=jnp.float32)
    return outputs


def body(queries, keys, values, rates, w_gate, w_up, w_down, gains, out_proj):
    group_count, local_rows, head_width = queries.shape
    first_device = lax.axis_index("ctx") == 0
    query_unit = unit_rows(queries.astype(jnp.float32))
    key_unit = unit_rows(keys.astype(jnp.float32))
    query_half = query_unit.astype(jnp.bfloat16)
    key_half = key_unit.astype(jnp.bfloat16)
    tails = jnp.stack([key_half[:, local_rows - WINDOW :], values[:, local_rows - WINDOW :]])
    prior = passed_along(tails, "ctx", 1)
    gate_now = w_gate[0]
    up_now = w_up[0]
    down_now = w_down[0]
    mixed = []
    for group_at in range(group_count):
        if group_at == 0:
            halo_rows = prior[:, 0]
            masked_head = first_device
        else:
            halo_rows = jnp.where(first_device, prior[:, group_at - 1], prior[:, group_at])
            masked_head = None
        ext_keys = jnp.concatenate([halo_rows[0], key_half[group_at]], axis=0)
        ext_values = jnp.concatenate([halo_rows[1], values[group_at]], axis=0)
        attended = band_attention(query_half[group_at], ext_keys, ext_values, masked_head)
        grads = fast_grads(
            key_unit[group_at],
            values[group_at].astype(jnp.float32),
            rates[0, group_at],
            gate_now,
            up_now,
            down_now,
        )
        ortho = orthogonal(lax.psum(grads, "ctx"))
        gate_now = gate_now + step_size * ortho[0]
        up_now = up_now + step_size * ortho[1]
        down_now = down_now + step_size * ortho[2].T
        fast_out = apply_fast(query_unit[group_at], gate_now, up_now, down_now)
        normed = (
            fast_out
            * lax.rsqrt(jnp.mean(fast_out * fast_out, axis=-1, keepdims=True) + 1e-05)
            * gains[0]
        )
        mixed.append((attended + normed).astype(jnp.bfloat16))
    combined = jnp.stack(mixed)
    proj_columns = lax.all_to_all(out_proj, "head", split_axis=1, concat_axis=0, tiled=True)
    summed = jnp.einsum(
        "ctf,fo->cto",
        lax.all_gather(combined, "head", axis=2, tiled=True),
        proj_columns,
        preferred_element_type=jnp.float32,
    )
    return summed.astype(jnp.bfloat16)


def solution(mesh):
    return jax.shard_map(
        body,
        mesh=mesh,
        in_specs=(
            P(None, "ctx", "head"),
            P(None, "ctx", "head"),
            P(None, "ctx", "head"),
            P("head", None, "ctx"),
            P("head", None, None),
            P("head", None, None),
            P("head", None, None),
            P("head", None),
            P("head", None),
        ),
        out_specs=P(None, "ctx", "head"),
        check_vma=False,
    )
```

profile of v0, /device:TPU:1, one launch (start us, length us, event | category | flops | bytes accessed | tf_op | source)
XLA Modules:
  0.0 370.9 jit_solution(8970687296122975035)
XLA Ops:
  10.1 3.6 collective-permute-start
  31.4 2.0 fusion.127
  33.4 82.0 %all-reduce.3.cloned.1.call-done = f32[3,256,512]{2,1,0:T(8,128)} async-done(((f32[3,256,512]{2,1,0:T(8,128)}), f32[3,256,512]{2,1,0:T(8,128)}) %all-reduce.3.cloned.1.call-update) | async-done | bytes 1572880 | tf_op jit(solution)/shard_map/psum | solution.py:116
  115.4 1.8 multiply_reduce_fusion.1
  117.3 1.8 fusion.85
  120.1 1.8 multiply_add_fusion.9
  121.9 1.7 fusion.128
  126.1 1.8 fusion.129
  130.4 1.7 fusion.130
  149.0 2.0 fusion.126
  153.2 1.9 multiply_reduce_fusion.3
  155.1 2.0 copy.11
  157.1 2.8 fusion.16
  159.9 83.1 %all-reduce.5.cloned.1.call-done = f32[3,256,512]{2,1,0:T(8,128)} async-done(((f32[3,256,512]{2,1,0:T(8,128)}), f32[3,256,512]{2,1,0:T(8,128)}) %all-reduce.5.cloned.1.call-update) | async-done | bytes 1572880 | tf_op jit(solution)/shard_map/psum | solution.py:116
  243.0 1.8 multiply_reduce_fusion
  244.9 1.8 fusion.86
  247.6 1.8 multiply_add_fusion.4
  252.1 1.8 multiply_add_fusion.3
  253.8 1.7 fusion.133
  264.8 1.8 multiply_add_fusion
  270.3 2.0 fusion.15
  273.4 43.4 %all_to_all.19 = bf16[256,16,256]{2,0,1:T(8,128)(2,1)S(1)} all-to-all(bf16[256,16,256]{2,0,1:T(8,128)(2,1)S(1)} %bitcast.208), channel_id=1, replica_groups=mesh['ctx'=8,'head'=16] {'head'}, dimensions={1} | all-to-all | bytes 4194304 | tf_op jit(solution)/shard_map/all_to_all | solution.py:128
  316.9 40.8 %all-gather.2.cloned.1.call-done = bf16[2,512,4096]{2,1,0:T(8,128)(2,1)} async-done(((bf16[2,512,256]{2,1,0:T(8,128)(2,1)}), bf16[2,512,4096]{2,1,0:T(8,128)(2,1)}) %all-gather.2.cloned.1.call-update) | async-done | bytes 8388624 | tf_op jit(solution)/shard_map/all_gather | solution.py:131
  357.6 6.5 %convolution_convert_fusion = bf16[2,512,256]{2,1,0:T(8,128)(2,1)} fusion(bf16[2,512,4096]{2,1,0:T(8,128)(2,1)} %all-gather.2.cloned.1.call-done, bf16[4096,256,1]{1,0,2:T(8,128)(2,1)S(1)} %bitcast.210), kind=kOutput, calls=%fused_computation.29 | convolution fusion | flops 2147745792 | bytes 11010048 | tf_op jit(solution)/shard_map/ctf,fo->cto/dot_general | solution.py:129
  (116 shorter events, 63.7 us)
Async XLA Ops:
  6.5 2.6 copy-start.5
  6.5 108.9 %all-reduce.3.cloned.1.call-start = ((), (), s32[]{:S(2)}) async-start(), calls=%async_computation.1 | async-start | bytes 3145728 | tf_op jit(solution)/shard_map/psum | solution.py:116
  9.1 4.5 %copy-start.21 = (f32[1,2,512]{2,1,0:T(2,128)S(1)}, f32[1,2,512]{2,1,0:T(2,128)}, u32[]{:S(2)}) copy-start(f32[1,2,512]{2,1,0:T(2,128)} %param.12) | copy-start | bytes 12292
  9.1 4.5 %copy-start = (f32[1,256,512]{2,1,0:T(8,128)S(1)}, f32[1,256,512]{2,1,0:T(8,128)}, u32[]{:S(2)}) copy-start(f32[1,256,512]{2,1,0:T(8,128)} %param.13) | copy-start | bytes 1572868
  9.2 5.5 %copy-start.8 = (f32[1,256,512]{2,1,0:T(8,128)S(1)}, f32[1,256,512]{2,1,0:T(8,128)}, u32[]{:S(2)}) copy-start(f32[1,256,512]{2,1,0:T(8,128)} %param.14) | copy-start | bytes 1572868
  10.1 17.9 %collective-permute-start = (bf16[2,2,256,256]{3,2,1,0:T(8,128)(2,1)}, bf16[2,2,256,256]{3,2,1,0:T(8,128)(2,1)}, u32[]{:S(2)}, u32[]{:S(2)}) collective-permute-start(bf16[2,2,256,256]{3,2,1,0:T(8,128)(2,1)} %pad_maximum_fusion.2), channel_id=1, source_target_pairs={{0,16},{16,32},{32,48},{48,64},{64,80},{80,96},{96,112},{112,0},{1... | collective-permute-start | bytes 1572872 | tf_op jit(solution)/shard_map/ppermute | solution.py:19
  22.1 2.7 copy-start.12
  22.2 220.8 %all-reduce.5.cloned.1.call-start = ((), (), s32[]{:S(2)}) async-start(), calls=%async_computation.2 | async-start | bytes 3145728 | tf_op jit(solution)/shard_map/psum | solution.py:116
  23.4 3.1 copy-start.13
  27.8 5.6 %copy-start.16 = (bf16[2,512,256]{2,1,0:T(8,128)(2,1)}, bf16[2,512,256]{2,1,0:T(8,128)(2,1)S(1)}, u32[]{:S(2)}) copy-start(bf16[2,512,256]{2,1,0:T(8,128)(2,1)S(1)} %get-tuple-element.6) | copy-start | bytes 1572868
  115.4 1.9 copy-start.14
  138.8 1.1 copy-start.9
  139.9 1.5 copy-start.1
  139.9 1.5 copy-start.6
  147.8 1.1 copy-start.18
  147.8 1.1 copy-start.20
  147.9 209.8 %all-gather.2.cloned.1.call-start = ((), (), s32[]{:S(2)}) async-start(), calls=%async_computation.3 | async-start | bytes 8912896 | tf_op jit(solution)/shard_map/all_gather | solution.py:131
  149.0 2.0 copy-start.3
  152.0 1.2 copy-start.2
  153.2 3.9 %copy-start.22 = (f32[1,256]{1,0:T(1,128)S(1)}, f32[1,256]{1,0:T(1,128)}, u32[]{:S(2)}) copy-start(f32[1,256]{1,0:T(1,128)} %param.16) | copy-start | bytes 3076
  243.0 1.9 copy-start.15
  264.8 1.8 copy-start.4
  270.3 2.0 copy-start.19
  270.3 2.9 copy-start.7
  (3 other events, 3.1 us)
Sparse Core Ops, SparseCore 0:
  22.3 93.0 all-reduce.2
  148.0 94.9 all-reduce.4
  273.3 84.2 all-gather.1
where the time goes:
time: 377 us; the launch traced here: 371 us
  waiting for transfers between devices  206 us (55%)
  matrix products  80.6 us (21%)
  blocking collectives  43.4 us (12%)
  other arithmetic  14 us (4%)
  between operations  14 us (4%)
  local copies, waits for them, and re-layouts  8.64 us (2%)
  starting transfers between devices  4.11 us (1%)
    psum x2, waiting for transfers between devices, body(): ortho = orthogonal(lax.psum(grads, 'ctx'))  165 us
    all_to_all x1, blocking collectives, body(): lax.all_to_all(out_proj, 'head', split_axis=1, concat_axis=0, tiled=True)  43.4 us
    all_gather x1, waiting for transfers between devices, body(): lax.all_gather(combined, 'head', axis=2, tiled=True)  40.8 us
    dot_general x18, matrix products, exact_dot(): jnp.dot(left, right, precision=highest, preferred_element_type=jnp.float32)  22.3 us
    dot_general x10, matrix products, orthogonal(): gram = jnp.einsum('mik,mjk->mij', iterate, iterate, precision=highest)  17 us
    dot_general x10, matrix products, quintic_step(): jnp.einsum('mij,mjk->mik', poly, iterate, precision=highest)  16.6 us
    dot_general x10, matrix products, quintic_step(): jnp.einsum('mij,mjk->mik', gram, gram, precision=highest)  9.34 us
  transfers between devices with their start and end apart: 4, of which 4 were waited for; matrix products, arithmetic and copies ran while one was open for 8% of the time, Pallas kernels for 0%

commit v1 on v0

--- a/solution.py
+++ b/solution.py
@@ -2,6 +2,7 @@
 import jax.numpy as jnp
 from jax import lax
 from jax.sharding import PartitionSpec as P
+from jax.lax import all_gather
 
 WINDOW = 256
 NS_ITERS = 5
@@ -126,9 +127,14 @@
         mixed.append((attended + normed).astype(jnp.bfloat16))
     combined = jnp.stack(mixed)
     proj_columns = lax.all_to_all(out_proj, "head", split_axis=1, concat_axis=0, tiled=True)
+
+    def view_screen(along_axis, vec):
+        r_now = jnp.concatenate(all_gather(vec, along_axis), 2)
+        return r_now
+
     summed = jnp.einsum(
         "ctf,fo->cto",
-        lax.all_gather(combined, "head", axis=2, tiled=True),
+        view_screen("head", combined),
         proj_columns,
         preferred_element_type=jnp.float32,
     )

time: 377 us -> 372 us (0.987)
  waiting for transfers between devices: 206 us -> 184 us
  blocking collectives: 43.4 us -> 54.5 us
  local copies, waits for them, and re-layouts: 8.64 us -> 13.8 us
    all_gather x1, waiting for transfers between devices: 40.8 us -> 18.6 us  [view_screen(): r_now = jnp.concatenate(all_gather(vec, along_axis), 2)]
    all_to_all x1, blocking collectives: 43.4 us -> 54.5 us  [body(): lax.all_to_all(out_proj, 'head', split_axis=1, concat_axis=0, tiled=True)]
  transfers between devices with their start and end apart: 4 -> 4, of which waited for: 4 -> 4; matrix products, arithmetic and copies ran while one was open for 8% -> 10% of each run, Pallas kernels for 0% -> 0%
where the time goes in v1:
time: 372 us; the launch traced here: 366 us
  waiting for transfers between devices  184 us (49%)
  matrix products  81 us (22%)
  blocking collectives  54.5 us (15%)
  between operations  14.2 us (4%)
  other arithmetic  14 us (4%)
  local copies, waits for them, and re-layouts  13.8 us (4%)
  starting transfers between devices  4.11 us (1%)
    psum x2, waiting for transfers between devices, body(): ortho = orthogonal(lax.psum(grads, 'ctx'))  165 us
    all_to_all x1, blocking collectives, body(): lax.all_to_all(out_proj, 'head', split_axis=1, concat_axis=0, tiled=True)  54.5 us
    dot_general x18, matrix products, exact_dot(): jnp.dot(left, right, precision=highest, preferred_element_type=jnp.float32)  22.3 us
    all_gather x1, waiting for transfers between devices, view_screen(): r_now = jnp.concatenate(all_gather(vec, along_axis), 2)  18.6 us
    dot_general x10, matrix products, orthogonal(): gram = jnp.einsum('mik,mjk->mij', iterate, iterate, precision=highest)  16.9 us
    dot_general x10, matrix products, quintic_step(): jnp.einsum('mij,mjk->mik', poly, iterate, precision=highest)  16.6 us
    dot_general x10, matrix products, quintic_step(): jnp.einsum('mij,mjk->mik', gram, gram, precision=highest)  9.34 us
  transfers between devices with their start and end apart: 4, of which 4 were waited for; matrix products, arithmetic and copies ran while one was open for 10% of the time, Pallas kernels for 0%

profile of v1, /device:TPU:1, one launch (start us, length us, event | category | flops | bytes accessed | tf_op | source)
XLA Modules:
  0.0 365.5 jit_solution(9011398698480807)
XLA Ops:
  10.1 3.6 collective-permute-start
  29.7 1.7 slice_bitcast_fusion.28
  31.4 2.0 fusion.135
  33.4 82.0 %all-reduce.3.cloned.1.call-done = f32[3,256,512]{2,1,0:T(8,128)} async-done(((f32[3,256,512]{2,1,0:T(8,128)}), f32[3,256,512]{2,1,0:T(8,128)}) %all-reduce.3.cloned.1.call-update) | async-done | bytes 1572880 | tf_op jit(solution)/shard_map/psum | solution.py:117
  115.4 1.8 multiply_reduce_fusion.1
  117.3 1.8 fusion.93
  120.0 1.8 multiply_add_fusion.9
  148.9 2.0 fusion.134
  153.2 1.9 multiply_reduce_fusion.3
  155.1 2.0 copy.21
  157.1 2.8 fusion.24
  159.9 83.1 %all-reduce.5.cloned.1.call-done = f32[3,256,512]{2,1,0:T(8,128)} async-done(((f32[3,256,512]{2,1,0:T(8,128)}), f32[3,256,512]{2,1,0:T(8,128)}) %all-reduce.5.cloned.1.call-update) | async-done | bytes 1572880 | tf_op jit(solution)/shard_map/psum | solution.py:117
  242.9 1.8 multiply_reduce_fusion
  244.8 1.8 fusion.94
  247.6 1.8 multiply_add_fusion.4
  252.0 1.8 multiply_add_fusion.3
  253.8 1.7 fusion.141
  264.8 1.8 multiply_add_fusion
  270.3 2.0 fusion.23
  273.2 2.5 copy.23
  275.7 2.8 copy.24
  278.6 54.5 %all_to_all.16 = bf16[256,16,256]{2,0,1:T(8,128)(2,1)} all-to-all(bf16[256,16,256]{2,0,1:T(8,128)(2,1)S(1)} %copy.24), channel_id=1, replica_groups=mesh['ctx'=8,'head'=16] {'head'}, dimensions={1} | all-to-all | bytes 4194304 | tf_op jit(solution)/shard_map/all_to_all | solution.py:129
  333.1 18.6 %all-gather.3.cloned.1.call-done = bf16[32,512,256]{2,1,0:T(8,128)(2,1)} async-done(((bf16[2,512,256]{2,1,0:T(8,128)(2,1)}), bf16[32,512,256]{2,1,0:T(8,128)(2,1)}) %all-gather.3.cloned.1.call-update) | async-done | bytes 8388624 | tf_op jit(solution)/shard_map/all_gather | solution.py:132
  351.7 7.1 %fusion.8 = bf16[2,512,256]{2,1,0:T(8,128)(2,1)} fusion(bf16[2,512,16,256]{3,1,0,2:T(8,128)(2,1)} %bitcast.222, bf16[256,16,256]{2,0,1:T(8,128)(2,1)} %all_to_all.16), kind=kOutput, calls=%fused_computation.31 | convolution fusion | flops 2147745792 | bytes 11010048 | tf_op jit(solution)/shard_map/ctf,fo->cto/dot_general | solution.py:135
  (115 shorter events, 66.8 us)
Async XLA Ops:
  6.5 2.6 copy-start.5
  6.5 108.8 %all-reduce.3.cloned.1.call-start = ((), (), s32[]{:S(2)}) async-start(), calls=%async_computation.1 | async-start | bytes 3145728 | tf_op jit(solution)/shard_map/psum | solution.py:117
  9.1 4.5 %copy-start.20 = (f32[1,2,512]{2,1,0:T(2,128)S(1)}, f32[1,2,512]{2,1,0:T(2,128)}, u32[]{:S(2)}) copy-start(f32[1,2,512]{2,1,0:T(2,128)} %param.12) | copy-start | bytes 12292
  9.1 4.5 %copy-start = (f32[1,256,512]{2,1,0:T(8,128)S(1)}, f32[1,256,512]{2,1,0:T(8,128)}, u32[]{:S(2)}) copy-start(f32[1,256,512]{2,1,0:T(8,128)} %param.13) | copy-start | bytes 1572868
  9.2 5.5 %copy-start.8 = (f32[1,256,512]{2,1,0:T(8,128)S(1)}, f32[1,256,512]{2,1,0:T(8,128)}, u32[]{:S(2)}) copy-start(f32[1,256,512]{2,1,0:T(8,128)} %param.14) | copy-start | bytes 1572868
  10.1 17.9 %collective-permute-start = (bf16[2,2,256,256]{3,2,1,0:T(8,128)(2,1)}, bf16[2,2,256,256]{3,2,1,0:T(8,128)(2,1)}, u32[]{:S(2)}, u32[]{:S(2)}) collective-permute-start(bf16[2,2,256,256]{3,2,1,0:T(8,128)(2,1)} %pad_maximum_fusion.2), channel_id=1, source_target_pairs={{0,16},{16,32},{32,48},{48,64},{64,80},{80,96},{96,112},{112,0},{1... | collective-permute-start | bytes 1572872 | tf_op jit(solution)/shard_map/ppermute | solution.py:20
  22.2 220.8 %all-reduce.5.cloned.1.call-start = ((), (), s32[]{:S(2)}) async-start(), calls=%async_computation.2 | async-start | bytes 3145728 | tf_op jit(solution)/shard_map/psum | solution.py:117
  23.4 3.1 copy-start.12
  27.8 5.6 %copy-start.15 = (bf16[2,512,256]{2,1,0:T(8,128)(2,1)}, bf16[2,512,256]{2,1,0:T(8,128)(2,1)S(1)}, u32[]{:S(2)}) copy-start(bf16[2,512,256]{2,1,0:T(8,128)(2,1)S(1)} %get-tuple-element.6) | copy-start | bytes 1572868
  115.4 1.9 copy-start.13
  138.8 1.1 copy-start.9
  139.9 1.5 copy-start.1
  139.9 1.5 copy-start.6
  147.8 1.1 copy-start.17
  147.8 1.1 copy-start.19
  147.8 203.8 %all-gather.3.cloned.1.call-start = ((), (), s32[]{:S(2)}) async-start(), calls=%async_computation.3 | async-start | bytes 8912896 | tf_op jit(solution)/shard_map/all_gather | solution.py:132
  148.9 2.0 copy-start.3
  150.9 1.1 copy-start.10
  152.0 1.2 copy-start.2
  153.2 4.0 %copy-start.21 = (f32[1,256]{1,0:T(1,128)S(1)}, f32[1,256]{1,0:T(1,128)}, u32[]{:S(2)}) copy-start(f32[1,256]{1,0:T(1,128)} %param.16) | copy-start | bytes 3076
  242.9 1.9 copy-start.14
  264.8 1.8 copy-start.4
  270.3 2.0 copy-start.18
  270.3 2.9 copy-start.7
  (2 other events, 2.1 us)
Sparse Core Ops, SparseCore 0:
  22.3 93.0 all-reduce.2
  148.0 94.9 all-reduce.4
  273.3 78.3 all-gather.2
